TPU v7x, 32 devices: a whole 2x2x4 slice. The times are simulated.
32 devices in a mesh: seg: 8 (over z, core), bond: 4 (over y, x).
Axes of the slice: x: 2, y: 2, z: 4, core: 2. Of those that a mesh axis runs over, the one named last changes fastest.
Arguments:
- left_env: bfloat16 [8, 1024, 6, 1024], P('seg', 'bond'), may hold values from -0.1875 to 0.1875
- prev_left: bfloat16 [8, 1024, 1024], P('seg'), may hold values from -0.25 to 1.25
- cur_site: bfloat16 [8, 1024, 4, 1024], P('seg', 'bond'), may hold values from -6 to 6
- prev_site: bfloat16 [8, 1024, 4, 1024], P('seg', None, None, 'bond'), may hold values from -6 to 6
- hamiltonian: bfloat16 [8, 6, 6, 4, 4], P('seg'), may hold values from -1.25 to 1.25
- right_env: bfloat16 [8, 1024, 6, 1024], P('seg', 'bond'), may hold values from -0.078125 to 0.078125
- prev_right: bfloat16 [8, 1024, 1024], P('seg'), may hold values from -0.25 to 1.25
Outputs:
- new_site: bfloat16 [8, 1024, 4, 1024], P('seg', 'bond')
- center: float32 [8, 1024, 1024], P('seg', 'bond')
All inputs are finite; a program needn't handle non-finite values.
Results may differ from a plain program's by a relative error of at most 0.0054.
Values may be sent and summed in bfloat16 or wider, within the bound.
A program may use at most 128 MiB of HBM per device.

v0:
```python
import math
import jax
import jax.numpy as jnp
from jax import lax
from jax.sharding import PartitionSpec as P

PHYS = 4
MPOB = 6


def shifted(block, axis, distance):
    devices = range(lax.axis_size(axis))
    route = [((i - distance) % len(devices), i) for i in devices]
    return lax.ppermute(block, axis, route)


def shards(left_env, prev_left, cur_site, prev_site, hamiltonian, right_env, prev_right):
    left_now, prev_now = shifted((left_env[0], prev_left[0]), "seg", 1)
    own_rows = left_now.shape[0]
    bond_width = left_now.shape[2]
    coupling = hamiltonian[0].astype(jnp.float32)
    current = lax.all_gather(cur_site[0], "bond", axis=0, tiled=True)
    projected = jnp.dot(
        left_now.reshape(own_rows * MPOB, bond_width),
        current.reshape(bond_width, PHYS * bond_width),
        preferred_element_type=jnp.float32,
    ).reshape(own_rows, MPOB, PHYS, bond_width)
    mixture = jnp.einsum(
        "autc,uvst->asvc", projected, coupling, precision=lax.Precision.HIGHEST
    ).astype(jnp.bfloat16)
    applied = jnp.einsum(
        "asvc,cvy->asy",
        mixture,
        lax.all_gather(right_env[0], "bond", axis=0, tiled=True),
        preferred_element_type=jnp.float32,
    )
    partial_value = jnp.einsum(
        "ab,bsc->asc", prev_now, prev_site[0], preferred_element_type=jnp.float32
    ).astype(jnp.bfloat16)
    second = jnp.einsum(
        "akc,cy->aky",
        lax.all_to_all(partial_value, "bond", split_axis=0, concat_axis=2, tiled=True),
        prev_right[0],
        preferred_element_type=jnp.float32,
    )
    target = (2.0 * applied - second).reshape(own_rows * PHYS, bond_width)
    local_correlation = jnp.dot(
        target.T, target, precision=lax.Precision.HIGHEST, preferred_element_type=jnp.float32
    )
    correlation = lax.psum(local_correlation, "bond")
    triangle = jnp.linalg.cholesky(correlation)
    solved = jax.scipy.linalg.solve_triangular(triangle, target.T, lower=True)
    norming = math.sqrt(bond_width * PHYS)
    new_site = (solved.T * norming).astype(jnp.bfloat16).reshape(1, own_rows, PHYS, bond_width)
    offset = lax.axis_index("bond") * own_rows
    center = lax.dynamic_slice_in_dim(triangle.T, offset, own_rows, 0) / norming
    return (new_site, center[None])


def solution(mesh):
    return jax.shard_map(
        shards,
        mesh=mesh,
        in_specs=(
            P("seg", "bond", None, None),
            P("seg", None, None),
            P("seg", "bond", None, None),
            P("seg", None, None, "bond"),
            P("seg", None, None, None, None),
            P("seg", "bond", None, None),
            P("seg", None, None),
        ),
        out_specs=(P("seg", "bond", None, None), P("seg", "bond", None)),
        check_vma=False,
    )
```

profile of v0, /device:TPU:0, one launch (start us, length us, event | category | flops | bytes accessed | tf_op | source)
XLA Modules:
  0.0 759.1 jit_solution(3926485406650583413)
XLA Ops:
  11.9 25.3 %collective-permute-done.1 = bf16[1024,1024]{1,0:T(8,128)(2,1)S(1)} collective-permute-done((bf16[1024,1024]{1,0:T(8,128)(2,1)}, bf16[1024,1024]{1,0:T(8,128)(2,1)S(1)}, u32[]{:S(2)}, u32[]{:S(2)}) %collective-permute-start.1) | collective-permute-done | bytes 2097184 | tf_op jit(solution)/shard_map/ppermute | solution.py:14
  41.2 40.1 %all_to_all.18 = bf16[1024,4,256]{2,1,0:T(4,128)(2,1)S(1)} all-to-all(bf16[1024,4,256]{2,1,0:T(4,128)(2,1)S(1)} %copy.30), channel_id=1, replica_groups=mesh['seg'=8,'bond'=4] {'bond'}, dimensions={0} | all-to-all | bytes 4194304 | tf_op jit(solution)/shard_map/all_to_all | solution.py:42
  92.1 22.9 %all-gather.5.cloned.1.call-done = bf16[1,1024,4,1024]{3,2,0,1:T(4,128)(2,1)} async-done(((bf16[1,256,4,1024]{3,2,0,1:T(4,128)(2,1)}), bf16[1,1024,4,1024]{3,2,0,1:T(4,128)(2,1)}) %all-gather.5.cloned.1.call-update) | async-done | bytes 8388624 | tf_op jit(solution)/shard_map/all_gather | solution.py:22
  115.0 14.1 %copy.45 = bf16[1,1024,4,1024]{1,3,2,0:T(8,128)(2,1)} copy(bf16[1,1024,4,1024]{3,2,0,1:T(4,128)(2,1)} %all-gather.5.cloned.1.call-done) | data formatting | bytes 16777216 | tf_op jit(solution)/shard_map/reshape | solution.py:25
  129.1 21.9 %convolution_bitcast_fusion = f32[256,6,4,1024,1]{3,0,2,1,4:T(8,128)} fusion(bf16[1,1024,4,1024]{1,3,2,0:T(8,128)(2,1)} %copy.45, bf16[256,6,1024]{2,0,1:T(8,128)(2,1)} %collective-permute-done), kind=kOutput, calls=%fused_computation.9 | convolution fusion | flops 12884901888 | bytes 36700160 | tf_op jit(solution)/shard_map/dot_general | solution.py:23
  151.0 62.8 %fusion.2 = bf16[256,4,6,1024]{3,2,1,0:T(8,128)(2,1)} fusion(f32[256,6,4,1024,1]{3,0,2,1,4:T(8,128)} %convolution_bitcast_fusion, bf16[1,6,6,4,4]{2,4,3,1,0:T(4,128)(2,1)S(1)} %copy-done.5), kind=kOutput, calls=%fused_computation.5 | convolution fusion | flops 1818230784 | bytes 37749888 | tf_op jit(solution)/shard_map/autc,uvst->asvc/dot_general | solution.py:28
  213.7 25.5 %all-gather.7.cloned.1.call-done = bf16[1,1024,6,1024]{3,1,2,0:T(8,128)(2,1)} async-done(((bf16[1,256,6,1024]{3,1,2,0:T(8,128)(2,1)}), bf16[1,1024,6,1024]{3,1,2,0:T(8,128)(2,1)}) %all-gather.7.cloned.1.call-update) | async-done | bytes 12582928 | tf_op jit(solution)/shard_map/all_gather | solution.py:34
  239.2 32.4 %fusion.10 = f32[256,4,1024]{2,0,1:T(8,128)S(1)} fusion(f32[256,4,1024]{2,0,1:T(8,128)} %fusion.26, bf16[1,1024,6,1024]{3,1,2,0:T(8,128)(2,1)} %all-gather.7.cloned.1.call-done, bf16[256,4,6,1024]{3,2,1,0:T(8,128)(2,1)} %fusion.2), kind=kOutput, calls=%fused_computation.14 | convolution fusion | flops 12886999040 | bytes 33554432 | tf_op jit(solution)/shard_map/asvc,cvy->asy/dot_general | solution.py:31
  273.6 15.1 %convolution_bitcast_fusion.1 = f32[1024,1024]{0,1:T(8,128)} fusion(f32[256,4,1024]{2,0,1:T(8,128)S(1)} %fusion.10), kind=kOutput, calls=%fused_computation.20 | convolution fusion | flops 12884901888 | bytes 8388608 | tf_op jit(solution)/shard_map/dot_general | solution.py:47
  306.4 86.1 %all-reduce.3.cloned.1.call-done = f32[1024,1024]{0,1:T(8,128)} async-done(((f32[1024,1024]{0,1:T(8,128)}), f32[1024,1024]{0,1:T(8,128)}) %all-reduce.3.cloned.1.call-update) | async-done | bytes 4194320 | tf_op jit(solution)/shard_map/psum | solution.py:50
  404.7 11.7 %cholesky.223 = f32[128,128]{1,0:T(8,128)S(1)} custom-call(f32[128,128]{1,0:T(8,128)S(1)} %cholesky.580), custom_call_target="Cholesky" | custom-call | tf_op jit(solution)/shard_map/jit(cholesky)/cholesky | solution.py:51
  416.4 9.8 %custom-call.63 = f32[1,128,128]{1,2,0:T(8,128)S(1)} custom-call(f32[1,128,128]{2,1,0:T(8,128)S(1)} %get-tuple-element.74), custom_call_target="InvertDiagBlocksLowerTriangular" | custom-call | tf_op jit(solution)/shard_map/jit(cholesky)/cholesky | solution.py:51
  432.7 11.9 %cholesky.244 = f32[128,128]{1,0:T(8,128)S(1)} custom-call(f32[128,128]{1,0:T(8,128)S(1)} %cholesky.584), custom_call_target="Cholesky" | custom-call | tf_op jit(solution)/shard_map/jit(cholesky)/cholesky | solution.py:51
  458.4 11.7 %cholesky.468 = f32[128,128]{1,0:T(8,128)S(1)} custom-call(f32[128,128]{1,0:T(8,128)S(1)} %cholesky.589), custom_call_target="Cholesky" | custom-call | tf_op jit(solution)/shard_map/jit(cholesky)/cholesky | solution.py:51
  471.4 9.8 %custom-call.65 = f32[1,128,128]{1,2,0:T(8,128)S(1)} custom-call(f32[1,128,128]{2,1,0:T(8,128)S(1)} %get-tuple-element.68), custom_call_target="InvertDiagBlocksLowerTriangular" | custom-call | tf_op jit(solution)/shard_map/jit(cholesky)/cholesky | solution.py:51
  484.7 11.9 %cholesky.487 = f32[128,128]{1,0:T(8,128)S(1)} custom-call(f32[128,128]{1,0:T(8,128)S(1)} %cholesky.594), custom_call_target="Cholesky" | custom-call | tf_op jit(solution)/shard_map/jit(cholesky)/cholesky | solution.py:51
  497.9 9.8 %custom-call.66 = f32[1,128,128]{1,2,0:T(8,128)S(1)} custom-call(f32[1,128,128]{2,1,0:T(8,128)S(1)} %get-tuple-element.65), custom_call_target="InvertDiagBlocksLowerTriangular" | custom-call | tf_op jit(solution)/shard_map/jit(cholesky)/cholesky | solution.py:51
  511.2 11.7 %cholesky.506 = f32[128,128]{1,0:T(8,128)S(1)} custom-call(f32[128,128]{1,0:T(8,128)S(1)} %cholesky.599), custom_call_target="Cholesky" | custom-call | tf_op jit(solution)/shard_map/jit(cholesky)/cholesky | solution.py:51
  524.2 10.2 %custom-call.67 = f32[1,128,128]{1,2,0:T(8,128)S(1)} custom-call(f32[1,128,128]{2,1,0:T(8,128)S(1)} %get-tuple-element.62), custom_call_target="InvertDiagBlocksLowerTriangular" | custom-call | tf_op jit(solution)/shard_map/jit(cholesky)/cholesky | solution.py:51
  537.7 11.7 %cholesky.526 = f32[128,128]{1,0:T(8,128)S(1)} custom-call(f32[128,128]{1,0:T(8,128)S(1)} %cholesky.604), custom_call_target="Cholesky" | custom-call | tf_op jit(solution)/shard_map/jit(cholesky)/cholesky | solution.py:51
  563.5 11.9 %cholesky.546 = f32[128,128]{1,0:T(8,128)S(1)} custom-call(f32[128,128]{1,0:T(8,128)S(1)} %cholesky.609), custom_call_target="Cholesky" | custom-call | tf_op jit(solution)/shard_map/jit(cholesky)/cholesky | solution.py:51
  589.0 11.7 %cholesky.564 = f32[128,128]{1,0:T(8,128)S(1)} custom-call(f32[128,128]{1,0:T(8,128)S(1)} %convolution_subtract_fusion.11), custom_call_target="Cholesky" | custom-call | tf_op jit(solution)/shard_map/jit(cholesky)/cholesky | solution.py:51
  614.3 23.0 %while.1 = (s32[]{:T(128)}, f32[1024,1024]{1,0:T(8,128)}, s32[8,2]{0,1:T(2,128)S(1)}, f32[8,128,128]{2,1,0:T(8,128)S(1)}, s32[]{:T(128)}) while((s32[]{:T(128)}, f32[1024,1024]{1,0:T(8,128)}, s32[8,2]{0,1:T(2,128)S(1)}, f32[8,128,128]{2,1,0:T(8,128)S(1)}, s32[]{:T(128)}) %tuple.65), condition=%wide.while_cond, body=%wide.while_body.sunk | while | flops 2 | bytes 131181 | solution.py:52
  637.3 78.8 %custom-call.70 = f32[8,128,128]{1,2,0:T(8,128)S(1)} custom-call(f32[8,128,128]{2,1,0:T(8,128)S(1)} %get-tuple-element.9), custom_call_target="InvertDiagBlocksLowerTriangular" | custom-call | tf_op jit(solution)/shard_map/jit(_solve_triangular)/triangular_solve | solution.py:52
  (119 shorter events, 180.9 us)
Async XLA Ops:
  7.2 30.0 %copy-start = (bf16[1,1024,4,256]{3,2,1,0:T(4,128)(2,1)S(1)}, bf16[1,1024,4,256]{3,2,1,0:T(4,128)(2,1)}, u32[]{:S(2)}) copy-start(bf16[1,1024,4,256]{3,2,1,0:T(4,128)(2,1)} %param.10) | copy-start | bytes 6291460
  7.2 107.8 %all-gather.5.cloned.1.call-start = ((), (), s32[]{:S(2)}) async-start(), calls=%async_computation.2 | async-start | bytes 10485760 | tf_op jit(solution)/shard_map/all_gather | solution.py:22
  7.9 231.3 %all-gather.7.cloned.1.call-start = ((), (), s32[]{:S(2)}) async-start(), calls=%async_computation.3 | async-start | bytes 15728640 | tf_op jit(solution)/shard_map/all_gather | solution.py:34
  8.7 383.9 %all-reduce.3.cloned.1.call-start = ((), (), s32[]{:S(2)}) async-start(), calls=%async_computation.1 | async-start | bytes 8388608 | tf_op jit(solution)/shard_map/psum | solution.py:50
  8.7 28.5 %collective-permute-start.1 = (bf16[1024,1024]{1,0:T(8,128)(2,1)}, bf16[1024,1024]{1,0:T(8,128)(2,1)S(1)}, u32[]{:S(2)}, u32[]{:S(2)}) collective-permute-start(bf16[1024,1024]{1,0:T(8,128)(2,1)} %bitcast.186), channel_id=1, source_target_pairs={{28,0},{0,4},{4,8},{8,12},{12,16},{16,20},{20,24},{24,28},{29,1},{... | collective-permute-start | bytes 6291464 | tf_op jit(solution)/shard_map/ppermute | solution.py:14
  9.3 119.9 %collective-permute-start = (bf16[256,6,1024]{2,0,1:T(8,128)(2,1)}, bf16[256,6,1024]{2,0,1:T(8,128)(2,1)}, u32[]{:S(2)}, u32[]{:S(2)}) collective-permute-start(bf16[256,6,1024]{2,0,1:T(8,128)(2,1)} %bitcast.185), channel_id=1, source_target_pairs={{28,0},{0,4},{4,8},{8,12},{12,16},{16,20},{20,24},{24,28},{29,1},{... | collective-permute-start | bytes 9437192 | tf_op jit(solution)/shard_map/ppermute | solution.py:14
  129.1 21.9 %copy-start.5 = (bf16[1,6,6,4,4]{2,4,3,1,0:T(4,128)(2,1)S(1)}, bf16[1,6,6,4,4]{2,4,3,1,0:T(4,128)(2,1)}, u32[]{:S(2)}) copy-start(bf16[1,6,6,4,4]{2,4,3,1,0:T(4,128)(2,1)} %param.11) | copy-start | bytes 3460
  271.7 1.9 copy-start.4
  402.7 2.0 copy-start.3
  716.2 4.3 copy-start.2
  741.5 10.8 %copy-start.1 = (bf16[1,1024,4,256]{3,2,1,0:T(4,128)(2,1)S(1)}, bf16[1,1024,4,256]{3,2,1,0:T(4,128)(2,1)}, u32[]{:S(2)}) copy-start(bf16[1,1024,4,256]{3,2,1,0:T(4,128)(2,1)} %param.10) | copy-start | bytes 6291460
Sparse Core Ops, SparseCore 0:
  9.8 105.0 all-gather.4
  116.8 122.3 all-gather.6
  288.9 103.5 all-reduce.2
where the time goes:
time: 764 us; the launch traced here: 759 us
  other arithmetic  265 us (35%)
  matrix products  187 us (24%)
  waiting for transfers between devices  161 us (21%)
  local copies, waits for them, and re-layouts  82.3 us (11%)
  blocking collectives  40.1 us (5%)
  between operations  19.3 us (3%)
    another operation x30, other arithmetic, shards(): triangle = jnp.linalg.cholesky(correlation)  172 us
    psum x1, waiting for transfers between devices, shards(): correlation = lax.psum(local_correlation, 'bond')  86.1 us
    another operation x3, other arithmetic, shards(): solved = jax.scipy.linalg.solve_triangular(triangle, target.T, lower=True)  85.5 us
    dot_general x1, matrix products, shards(): jnp.einsum('autc,uvst->asvc', projected, coupling, precision=lax.Precisio...  62.8 us
    all_to_all x1, blocking collectives, shards(): lax.all_to_all(partial_value, 'bond', split_axis=0, concat_axis=2, tiled=...  40.1 us
    dot_general x1, matrix products, shards(): jnp.einsum('asvc,cvy->asy', mixture, lax.all_gather(right_env[0], 'bond',...  32.4 us
    all_gather x1, waiting for transfers between devices, shards(): lax.all_gather(right_env[0], 'bond', axis=0, tiled=True)  25.5 us
    ppermute x2, waiting for transfers between devices, shifted(): return lax.ppermute(block, axis, route)  25.3 us
  transfers between devices with their start and end apart: 5, of which 4 were waited for; matrix products, arithmetic and copies ran while one was open for 17% of the time, Pallas kernels for 0%

commit v1 on v0

--- a/solution.py
+++ b/solution.py
@@ -3,6 +3,7 @@
 import jax.numpy as jnp
 from jax import lax
 from jax.sharding import PartitionSpec as P
+from jax.lax import all_gather
 
 PHYS = 4
 MPOB = 6
@@ -47,7 +48,7 @@
     local_correlation = jnp.dot(
         target.T, target, precision=lax.Precision.HIGHEST, preferred_element_type=jnp.float32
     )
-    correlation = lax.psum(local_correlation, "bond")
+    correlation = all_gather(local_correlation, "bond").sum(axis=0)
     triangle = jnp.linalg.cholesky(correlation)
     solved = jax.scipy.linalg.solve_triangular(triangle, target.T, lower=True)
     norming = math.sqrt(bond_width * PHYS)

time: 764 us -> 828 us (1.084)
  waiting for transfers between devices: 161 us -> 214 us
  other arithmetic: 265 us -> 276 us
    all_gather x0 -> x1, waiting for transfers between devices: none -> 139 us  [shards(): correlation = all_gather(local_correlation, 'bond').sum(axis=0)]
    psum x1 -> x0, waiting for transfers between devices: 86.1 us -> none  [shards(): correlation = lax.psum(local_correlation, 'bond')]
    reduce_sum x0 -> x1, other arithmetic: none -> 10.3 us  [shards(): correlation = all_gather(local_correlation, 'bond').sum(axis=0)]
  transfers between devices with their start and end apart: 5 -> 5, of which waited for: 4 -> 4; matrix products, arithmetic and copies ran while one was open for 17% -> 16% of each run, Pallas kernels for 0% -> 0%
where the time goes in v1:
time: 828 us; the launch traced here: 823 us
  other arithmetic  276 us (33%)
  waiting for transfers between devices  214 us (26%)
  matrix products  187 us (23%)
  local copies, waits for them, and re-layouts  82.5 us (10%)
  blocking collectives  40.1 us (5%)
  between operations  19.4 us (2%)
    another operation x30, other arithmetic, shards(): triangle = jnp.linalg.cholesky(correlation)  172 us
    all_gather x1, waiting for transfers between devices, shards(): correlation = all_gather(local_correlation, 'bond').sum(axis=0)  139 us
    another operation x3, other arithmetic, shards(): solved = jax.scipy.linalg.solve_triangular(triangle, target.T, lower=True)  85.4 us
    dot_general x1, matrix products, shards(): jnp.einsum('autc,uvst->asvc', projected, coupling, precision=lax.Precisio...  62.9 us
    all_to_all x1, blocking collectives, shards(): lax.all_to_all(partial_value, 'bond', split_axis=0, concat_axis=2, tiled=...  40.1 us
    dot_general x1, matrix products, shards(): jnp.einsum('asvc,cvy->asy', mixture, lax.all_gather(right_env[0], 'bond',...  32.4 us
    all_gather x1, waiting for transfers between devices, shards(): lax.all_gather(right_env[0], 'bond', axis=0, tiled=True)  25.4 us
    ppermute x2, waiting for transfers between devices, shifted(): return lax.ppermute(block, axis, route)  25.3 us
  transfers between devices with their start and end apart: 5, of which 4 were waited for; matrix products, arithmetic and copies ran while one was open for 16% of the time, Pallas kernels for 0%

profile of v1, /device:TPU:0, one launch (start us, length us, event | category | flops | bytes accessed | tf_op | source)
XLA Modules:
  0.0 822.7 jit_solution(15423488302968876077)
XLA Ops:
  11.9 25.3 %collective-permute-done.1 = bf16[1024,1024]{1,0:T(8,128)(2,1)S(1)} collective-permute-done((bf16[1024,1024]{1,0:T(8,128)(2,1)}, bf16[1024,1024]{1,0:T(8,128)(2,1)S(1)}, u32[]{:S(2)}, u32[]{:S(2)}) %collective-permute-start.1) | collective-permute-done | bytes 2097184 | tf_op jit(solution)/shard_map/ppermute | solution.py:15
  41.2 40.1 %all_to_all.18 = bf16[1024,4,256]{2,1,0:T(4,128)(2,1)S(1)} all-to-all(bf16[1024,4,256]{2,1,0:T(4,128)(2,1)S(1)} %copy.28), channel_id=1, replica_groups=mesh['seg'=8,'bond'=4] {'bond'}, dimensions={0} | all-to-all | bytes 4194304 | tf_op jit(solution)/shard_map/all_to_all | solution.py:43
  92.1 22.9 %all-gather.7.cloned.1.call-done = bf16[1,1024,4,1024]{3,2,0,1:T(4,128)(2,1)} async-done(((bf16[1,256,4,1024]{3,2,0,1:T(4,128)(2,1)}), bf16[1,1024,4,1024]{3,2,0,1:T(4,128)(2,1)}) %all-gather.7.cloned.1.call-update) | async-done | bytes 8388624 | tf_op jit(solution)/shard_map/all_gather | solution.py:23
  115.0 14.1 %copy.41 = bf16[1,1024,4,1024]{1,3,2,0:T(8,128)(2,1)} copy(bf16[1,1024,4,1024]{3,2,0,1:T(4,128)(2,1)} %all-gather.7.cloned.1.call-done) | data formatting | bytes 16777216 | tf_op jit(solution)/shard_map/reshape | solution.py:26
  129.1 21.9 %convolution_bitcast_fusion = f32[256,6,4,1024,1]{3,0,2,1,4:T(8,128)} fusion(bf16[1,1024,4,1024]{1,3,2,0:T(8,128)(2,1)} %copy.41, bf16[256,6,1024]{2,0,1:T(8,128)(2,1)} %collective-permute-done), kind=kOutput, calls=%fused_computation.9 | convolution fusion | flops 12884901888 | bytes 36700160 | tf_op jit(solution)/shard_map/dot_general | solution.py:24
  151.0 62.9 %fusion.2 = bf16[256,4,6,1024]{3,2,1,0:T(8,128)(2,1)} fusion(f32[256,6,4,1024,1]{3,0,2,1,4:T(8,128)} %convolution_bitcast_fusion, bf16[1,6,6,4,4]{2,4,3,1,0:T(4,128)(2,1)S(1)} %copy-done.5), kind=kOutput, calls=%fused_computation.5 | convolution fusion | flops 1818230784 | bytes 37749888 | tf_op jit(solution)/shard_map/autc,uvst->asvc/dot_general | solution.py:29
  213.8 25.4 %all-gather.9.cloned.1.call-done = bf16[1,1024,6,1024]{3,1,2,0:T(8,128)(2,1)} async-done(((bf16[1,256,6,1024]{3,1,2,0:T(8,128)(2,1)}), bf16[1,1024,6,1024]{3,1,2,0:T(8,128)(2,1)}) %all-gather.9.cloned.1.call-update) | async-done | bytes 12582928 | tf_op jit(solution)/shard_map/all_gather | solution.py:35
  239.2 32.4 %fusion.10 = f32[256,4,1024]{2,0,1:T(8,128)S(1)} fusion(f32[256,4,1024]{2,0,1:T(8,128)} %fusion.26, bf16[1,1024,6,1024]{3,1,2,0:T(8,128)(2,1)} %all-gather.9.cloned.1.call-done, bf16[256,4,6,1024]{3,2,1,0:T(8,128)(2,1)} %fusion.2), kind=kOutput, calls=%fused_computation.14 | convolution fusion | flops 12886999040 | bytes 33554432 | tf_op jit(solution)/shard_map/asvc,cvy->asy/dot_general | solution.py:32
  273.6 15.1 %convolution_bitcast_fusion.1 = f32[1024,1024]{1,0:T(8,128)} fusion(f32[256,4,1024]{2,0,1:T(8,128)S(1)} %fusion.10), kind=kOutput, calls=%fused_computation.20 | convolution fusion | flops 12884901888 | bytes 8388608 | tf_op jit(solution)/shard_map/dot_general | solution.py:48
  307.1 139.0 %all-gather.11.cloned.1.call-done = f32[4096,1024]{1,0:T(8,128)} async-done(((f32[1024,1024]{1,0:T(8,128)}), f32[4096,1024]{1,0:T(8,128)}) %all-gather.11.cloned.1.call-update) | async-done | bytes 16777232 | tf_op jit(solution)/shard_map/all_gather | solution.py:51
  446.2 10.3 %reduce_sum.9 = f32[1024,1024]{1,0:T(8,128)} reduce(f32[4,1024,1024]{2,1,0:T(8,128)} %bitcast.175, f32[]{:T(128)} %constant.278.clone.1), dimensions={0}, to_apply=%region_0.0 | reduce | flops 3145728 | bytes 20971524 | tf_op jit(solution)/shard_map/reduce_sum | solution.py:51
  468.6 11.7 %cholesky.223 = f32[128,128]{1,0:T(8,128)S(1)} custom-call(f32[128,128]{1,0:T(8,128)S(1)} %cholesky.580), custom_call_target="Cholesky" | custom-call | tf_op jit(solution)/shard_map/jit(cholesky)/cholesky | solution.py:52
  482.9 9.8 %custom-call.63 = f32[1,128,128]{1,2,0:T(8,128)S(1)} custom-call(f32[1,128,128]{2,1,0:T(8,128)S(1)} %get-tuple-element.74), custom_call_target="InvertDiagBlocksLowerTriangular" | custom-call | tf_op jit(solution)/shard_map/jit(cholesky)/cholesky | solution.py:52
  496.6 11.9 %cholesky.244 = f32[128,128]{1,0:T(8,128)S(1)} custom-call(f32[128,128]{1,0:T(8,128)S(1)} %cholesky.584), custom_call_target="Cholesky" | custom-call | tf_op jit(solution)/shard_map/jit(cholesky)/cholesky | solution.py:52
  509.1 9.8 %custom-call.64 = f32[1,128,128]{1,2,0:T(8,128)S(1)} custom-call(f32[1,128,128]{2,1,0:T(8,128)S(1)} %get-tuple-element.71), custom_call_target="InvertDiagBlocksLowerTriangular" | custom-call | tf_op jit(solution)/shard_map/jit(cholesky)/cholesky | solution.py:52
  522.3 11.7 %cholesky.468 = f32[128,128]{1,0:T(8,128)S(1)} custom-call(f32[128,128]{1,0:T(8,128)S(1)} %cholesky.589), custom_call_target="Cholesky" | custom-call | tf_op jit(solution)/shard_map/jit(cholesky)/cholesky | solution.py:52
  548.6 11.9 %cholesky.487 = f32[128,128]{1,0:T(8,128)S(1)} custom-call(f32[128,128]{1,0:T(8,128)S(1)} %cholesky.594), custom_call_target="Cholesky" | custom-call | tf_op jit(solution)/shard_map/jit(cholesky)/cholesky | solution.py:52
  575.1 11.7 %cholesky.506 = f32[128,128]{1,0:T(8,128)S(1)} custom-call(f32[128,128]{1,0:T(8,128)S(1)} %cholesky.599), custom_call_target="Cholesky" | custom-call | tf_op jit(solution)/shard_map/jit(cholesky)/cholesky | solution.py:52
  588.2 10.2 %custom-call.67 = f32[1,128,128]{1,2,0:T(8,128)S(1)} custom-call(f32[1,128,128]{2,1,0:T(8,128)S(1)} %get-tuple-element.62), custom_call_target="InvertDiagBlocksLowerTriangular" | custom-call | tf_op jit(solution)/shard_map/jit(cholesky)/cholesky | solution.py:52
  601.7 11.7 %cholesky.526 = f32[128,128]{1,0:T(8,128)S(1)} custom-call(f32[128,128]{1,0:T(8,128)S(1)} %cholesky.604), custom_call_target="Cholesky" | custom-call | tf_op jit(solution)/shard_map/jit(cholesky)/cholesky | solution.py:52
  627.5 11.9 %cholesky.546 = f32[128,128]{1,0:T(8,128)S(1)} custom-call(f32[128,128]{1,0:T(8,128)S(1)} %cholesky.609), custom_call_target="Cholesky" | custom-call | tf_op jit(solution)/shard_map/jit(cholesky)/cholesky | solution.py:52
  653.0 11.7 %cholesky.564 = f32[128,128]{1,0:T(8,128)S(1)} custom-call(f32[128,128]{1,0:T(8,128)S(1)} %convolution_subtract_fusion.11), custom_call_target="Cholesky" | custom-call | tf_op jit(solution)/shard_map/jit(cholesky)/cholesky | solution.py:52
  678.3 22.6 %while.1 = (s32[]{:T(128)}, f32[1024,1024]{1,0:T(8,128)}, s32[8,2]{0,1:T(2,128)S(1)}, f32[8,128,128]{2,1,0:T(8,128)S(1)}, s32[]{:T(128)}) while((s32[]{:T(128)}, f32[1024,1024]{1,0:T(8,128)}, s32[8,2]{0,1:T(2,128)S(1)}, f32[8,128,128]{2,1,0:T(8,128)S(1)}, s32[]{:T(128)}) %tuple.65), condition=%wide.while_cond, body=%wide.while_body.sunk | while | flops 2 | bytes 131181 | solution.py:53
  700.9 78.8 %custom-call.70 = f32[8,128,128]{1,2,0:T(8,128)S(1)} custom-call(f32[8,128,128]{2,1,0:T(8,128)S(1)} %get-tuple-element.9), custom_call_target="InvertDiagBlocksLowerTriangular" | custom-call | tf_op jit(solution)/shard_map/jit(_solve_triangular)/triangular_solve | solution.py:53
  (120 shorter events, 191.0 us)
Async XLA Ops:
  7.2 30.0 %copy-start = (bf16[1,1024,4,256]{3,2,1,0:T(4,128)(2,1)S(1)}, bf16[1,1024,4,256]{3,2,1,0:T(4,128)(2,1)}, u32[]{:S(2)}) copy-start(bf16[1,1024,4,256]{3,2,1,0:T(4,128)(2,1)} %param.10) | copy-start | bytes 6291460
  7.2 107.8 %all-gather.7.cloned.1.call-start = ((), (), s32[]{:S(2)}) async-start(), calls=%async_computation.1 | async-start | bytes 10485760 | tf_op jit(solution)/shard_map/all_gather | solution.py:23
  7.9 231.3 %all-gather.9.cloned.1.call-start = ((), (), s32[]{:S(2)}) async-start(), calls=%async_computation.2 | async-start | bytes 15728640 | tf_op jit(solution)/shard_map/all_gather | solution.py:35
  8.7 437.5 %all-gather.11.cloned.1.call-start = ((), (), s32[]{:S(2)}) async-start(), calls=%async_computation.3 | async-start | bytes 20971520 | tf_op jit(solution)/shard_map/all_gather | solution.py:51
  8.7 28.5 %collective-permute-start.1 = (bf16[1024,1024]{1,0:T(8,128)(2,1)}, bf16[1024,1024]{1,0:T(8,128)(2,1)S(1)}, u32[]{:S(2)}, u32[]{:S(2)}) collective-permute-start(bf16[1024,1024]{1,0:T(8,128)(2,1)} %bitcast.188), channel_id=1, source_target_pairs={{28,0},{0,4},{4,8},{8,12},{12,16},{16,20},{20,24},{24,28},{29,1},{... | collective-permute-start | bytes 6291464 | tf_op jit(solution)/shard_map/ppermute | solution.py:15
  9.3 119.9 %collective-permute-start = (bf16[256,6,1024]{2,0,1:T(8,128)(2,1)}, bf16[256,6,1024]{2,0,1:T(8,128)(2,1)}, u32[]{:S(2)}, u32[]{:S(2)}) collective-permute-start(bf16[256,6,1024]{2,0,1:T(8,128)(2,1)} %bitcast.187), channel_id=1, source_target_pairs={{28,0},{0,4},{4,8},{8,12},{12,16},{16,20},{20,24},{24,28},{29,1},{... | collective-permute-start | bytes 9437192 | tf_op jit(solution)/shard_map/ppermute | solution.py:15
  129.1 21.9 %copy-start.5 = (bf16[1,6,6,4,4]{2,4,3,1,0:T(4,128)(2,1)S(1)}, bf16[1,6,6,4,4]{2,4,3,1,0:T(4,128)(2,1)}, u32[]{:S(2)}) copy-start(bf16[1,6,6,4,4]{2,4,3,1,0:T(4,128)(2,1)} %param.11) | copy-start | bytes 3460
  271.7 1.9 copy-start.4
  466.7 1.9 copy-start.3
  779.7 4.3 copy-start.2
  805.1 10.8 %copy-start.1 = (bf16[1,1024,4,256]{3,2,1,0:T(4,128)(2,1)S(1)}, bf16[1,1024,4,256]{3,2,1,0:T(4,128)(2,1)}, u32[]{:S(2)}) copy-start(bf16[1,1024,4,256]{3,2,1,0:T(4,128)(2,1)} %param.10) | copy-start | bytes 6291460
Sparse Core Ops, SparseCore 0:
  9.8 105.0 all-gather.6
  116.8 122.3 all-gather.8
  288.9 157.2 all-gather.10
